TPU v7x, 32 devices: a whole 2x2x4 slice. The times are simulated.
32 devices in a mesh: gx: 4 (over y, core), gy: 8 (over z, x).
Axes of the slice: x: 2, y: 2, z: 4, core: 2. Of those that a mesh axis runs over, the one named last changes fastest.
Arguments:
- depth: float32 [16, 64, 1024], P(None, 'gx', 'gy'), may hold values from 0.5 to 2
- momentum: float32 [3, 16, 64, 1024], P(None, None, 'gx', 'gy'), may hold values from -2.5 to 2.5
- tracer: float32 [16, 64, 1024], P(None, 'gx', 'gy'), may hold values from -6 to 6
- cell_wet: int32 [64, 1024], P('gx', 'gy'), may hold values 0 or 1
- tile_wet: int32 [1, 8], replicated, may hold values 0 or 1
Outputs:
- new_depth: float32 [16, 64, 1024], P(None, 'gx', 'gy')
- new_momentum: float32 [3, 16, 64, 1024], P(None, None, 'gx', 'gy')
- new_tracer: float32 [16, 64, 1024], P(None, 'gx', 'gy')
All inputs are finite; a program needn't handle non-finite values. No bound on the sum of `cell_wet` on one device may be relied on, other than what follows from the above.
Results may differ from a plain program's by a relative error of at most 0.0003.
Values sent between devices are 32-bit elements; how exact they have to be, the bound alone decides.
A program may use at most 64 MiB of HBM per device.

v0:
```python
import functools

import jax
import jax.numpy as jnp
from jax import lax
from jax.experimental import pallas as pl
from jax.experimental.pallas import tpu as pltpu
from jax.sharding import PartitionSpec as P

ITERS = 3
TILE = 128
REACH = 2 * 3 + 1 + ITERS
SEG = 11

gravity = 9.81
time_step = 0.025
MESH = pl.DeviceIdType.MESH


def minmod(a, b):
    return jnp.maximum(jnp.minimum(a, b), 0.0) + jnp.minimum(jnp.maximum(a, b), 0.0)


def hll(left, right, weight, normal):
    hl, hr = left[0], right[0]
    ul, ur = left[normal] / hl, right[normal] / hr
    al, ar = jnp.sqrt(gravity * hl), jnp.sqrt(gravity * hr)
    lower = jnp.minimum(jnp.minimum(ul - al, ur - ar), 0.0)
    upper = jnp.maximum(jnp.maximum(ul + al, ur + ar), 0.0)
    scale = weight / (upper - lower)
    low, high = lower * scale, upper * scale
    take_left = high * (ul - lower)
    take_right = low * (upper - ur)
    flux = [take_left * l + take_right * r for l, r in zip(left, right)]
    flux[normal] = flux[normal] + (0.5 * gravity) * (high * hl * hl - low * hr * hr)
    return flux


def lane_next(x):
    return pltpu.roll(x, x.shape[-1] - 1, 1)


def lane_prev(x):
    return pltpu.roll(x, 1, 1)


def kernel(
    nx, ny, rows, cols, layers,
    tile_ref, depth_ref, mom_ref, tracer_ref, wet_ref,
    depth_out, mom_out, tracer_out,
    fa, fb, fc, wet, pack_l, pack_r, halo_l, halo_r,
    ce, cn, up, inv, z0, z1, z2, part, gather_x, gather_y,
    send_row, recv_row, send_wet, recv_wet, send_col, recv_col,
    send_cor, recv_cor, send_gx, recv_gx, send_gy, recv_gy,
):
    R = REACH
    high_rows = rows + 2 * R
    width = 2 * cols
    half = layers // 2
    gx, gy = lax.axis_index("gx"), lax.axis_index("gy")

    fa[...] = jnp.zeros_like(fa)
    wet[...] = jnp.zeros_like(wet)
    halo_l[...] = jnp.zeros_like(halo_l)
    halo_r[...] = jnp.zeros_like(halo_r)

    barrier = pltpu.get_barrier_semaphore()
    has = {-1: gx > 0, 1: gx < nx - 1}
    side = {-1: gy > 0, 1: gy < ny - 1}
    for o in range(1, nx):
        pl.semaphore_signal(barrier, inc=1, device_id=(lax.rem(gx + o, nx), gy), device_id_type=MESH)
    for o in range(1, ny):
        pl.semaphore_signal(barrier, inc=1, device_id=(gx, lax.rem(gy + o, ny)), device_id_type=MESH)
    for dx in (-1, 1):
        for dy in (-1, 1):
            @pl.when(jnp.logical_and(has[dx], side[dy]))
            def _(dx=dx, dy=dy):
                pl.semaphore_signal(barrier, inc=1, device_id=(gx + dx, gy + dy), device_id_type=MESH)

    tile = tile_ref[(gx * rows) // TILE, (gy * cols) // TILE].astype(jnp.float32)
    for r in range(rows):
        wet[R + r, :, :cols] = wet_ref[r : r + 1, :].astype(jnp.float32) * tile

    def load_row(r, carry):
        at = pl.ds(r, layers, stride=rows)
        fa[0, R + r, :, :cols] = depth_ref[at, :]
        for n in range(3):
            fa[1 + n, R + r, :, :cols] = mom_ref[n, at, :]
        fa[4, R + r, :, :cols] = tracer_ref[at, :]
        return carry

    lax.fori_loop(0, rows, load_row, 0)

    lane = lax.broadcasted_iota(jnp.int32, (half, cols), 1)

    def pack_row(r, carry):
        left = jnp.zeros((half, cols), jnp.float32)
        right = left
        for s in range(11):
            if s < 10:
                x = fa[s % 5, R + r, (s // 5) * half : (s // 5 + 1) * half, :cols]
            else:
                x = jnp.broadcast_to(wet[R + r, :, :cols], (half, cols))
            mask = jnp.logical_and(lane >= SEG * s, lane < SEG * s + R)
            left = jnp.where(mask, pltpu.roll(x, SEG * s, 1) if s else x, left)
            right = jnp.where(mask, pltpu.roll(x, (SEG * s + R) % cols, 1), right)
        pack_l[r] = left
        pack_r[r] = right
        return carry

    lax.fori_loop(0, rows, pack_row, 0)

    as_int = lambda flag: flag.astype(jnp.int32)
    corners = (as_int(has[-1]) + as_int(has[1])) * (as_int(side[-1]) + as_int(side[1]))
    pl.semaphore_wait(barrier, nx - 1 + ny - 1 + corners)

    copies = []
    mine = {-1: R, 1: rows}
    theirs = {-1: R + rows, 1: 0}
    pack = {-1: pack_l, 1: pack_r}
    halo = {-1: halo_r, 1: halo_l}
    for i, dx in enumerate((-1, 1)):
        for src, send, recv in ((fa, send_row, recv_row), (wet, send_wet, recv_wet)):
            if src is fa:
                a = fa.at[:, pl.ds(mine[dx], R), :, pl.ds(0, cols)]
                b = fa.at[:, pl.ds(theirs[dx], R), :, pl.ds(0, cols)]
            else:
                a = wet.at[pl.ds(mine[dx], R), :, pl.ds(0, cols)]
                b = wet.at[pl.ds(theirs[dx], R), :, pl.ds(0, cols)]
            send_to = pltpu.make_async_remote_copy(
                src_ref=a, dst_ref=b, send_sem=send.at[i], recv_sem=recv.at[i],
                device_id=(gx + dx, gy), device_id_type=MESH)
            come = pltpu.make_async_remote_copy(
                src_ref=a, dst_ref=b, send_sem=send.at[i], recv_sem=recv.at[1 - i],
                device_id=(gx + dx, gy), device_id_type=MESH)
            copies.append((has[dx], send_to, come))
    for j, dy in enumerate((-1, 1)):
        args = dict(src_ref=pack[dy], dst_ref=halo[dy].at[pl.ds(R, rows)], send_sem=send_col.at[j],
                    device_id=(gx, gy + dy), device_id_type=MESH)
        copies.append((side[dy],
                       pltpu.make_async_remote_copy(recv_sem=recv_col.at[j], **args),
                       pltpu.make_async_remote_copy(recv_sem=recv_col.at[1 - j], **args)))
        for i, dx in enumerate((-1, 1)):
            args = dict(src_ref=pack[dy].at[pl.ds(mine[dx] - R, R)],
                        dst_ref=halo[dy].at[pl.ds(theirs[dx], R)],
                        send_sem=send_cor.at[i, j],
                        device_id=(gx + dx, gy + dy), device_id_type=MESH)
            copies.append((jnp.logical_and(has[dx], side[dy]),
                           pltpu.make_async_remote_copy(recv_sem=recv_cor.at[i, j], **args),
                           pltpu.make_async_remote_copy(recv_sem=recv_cor.at[1 - i, 1 - j], **args)))
    for cond, go, come in copies:
        @pl.when(cond)
        def _(go=go):
            go.start()
    for cond, go, come in copies:
        @pl.when(cond)
        def _(go=go, come=come):
            go.wait_send()
            come.wait_recv()

    def unpack_row(r, carry):
        fr, fl = halo_r[r], halo_l[r]
        for s in range(11):
            a = pltpu.roll(fr, cols - SEG * s, 1) if s else fr
            b = pltpu.roll(fl, cols - R - SEG * s if SEG * s + R < cols else 2 * cols - R - SEG * s, 1)
            x = jnp.where(lane < R, a, jnp.where(lane >= cols - R, b, 0.0))
            if s < 10:
                fa[s % 5, r, (s // 5) * half : (s // 5 + 1) * half, cols:] = x
            else:
                wet[r, :, cols:] = x[:1]
        return carry

    lax.fori_loop(0, high_rows, unpack_row, 0)

    def transport(src, dst, lo, hi, keep):
        for part_of in range(2):
            cut = slice(part_of * half, (part_of + 1) * half)

            def usable(r):
                w = wet[r]
                u = [src[f, r, cut, :] for f in range(5)]
                u[0] = u[0] * w + (1.0 - w)
                return u

            def sides(u, before, after):
                s = [0.5 * minmod(b, a) for b, a in zip(before, after)]
                return [x - y for x, y in zip(u, s)], [x + y for x, y in zip(u, s)]

            def row_face(i, left):
                here, mid, far = usable(i), usable(i + 1), usable(i + 2)
                right, following = sides(
                    mid, [m - h for m, h in zip(mid, here)], [f - m for f, m in zip(far, mid)])
                return hll(left, right, wet[i] * wet[i + 1], 1), following

            def step(i, carry):
                flux_low, left = carry
                flux_high, following = row_face(i, left)
                u = usable(i)
                d = [lane_next(x) - x for x in u]
                right, left_c = sides(u, [lane_prev(x) for x in d], d)
                w = wet[i]
                across = hll(left_c, [lane_next(x) for x in right], w * lane_next(jnp.broadcast_to(w, (half, width))), 2)
                for f in range(5):
                    rate = -time_step * (flux_high[f] - flux_low[f] + (across[f] - lane_prev(across[f])))
                    old = src[f, i, cut, :]
                    if keep is None:
                        new = old + rate
                    elif keep == 0.75:
                        new = 0.75 * fa[f, i, cut, :] + 0.25 * (old + rate)
                    else:
                        new = fa[f, i, cut, :] * (1.0 / 3.0) + (2.0 / 3.0) * (old + rate)
                    dst[f, i, cut, :] = new
                return flux_high, following

            a, b, c = usable(lo - 2), usable(lo - 1), usable(lo)
            _, left = sides(b, [y - x for x, y in zip(a, b)], [y - x for x, y in zip(b, c)])
            flux, left = row_face(lo - 1, left)
            lax.fori_loop(lo, hi, step, (flux, left))

    transport(fa, fb, 2, high_rows - 2, None)
    transport(fb, fc, 4, high_rows - 4, 0.75)
    transport(fc, fb, 6, high_rows - 6, 1.0 / 3.0)

    layer_id = lax.broadcasted_iota(jnp.int32, (layers, width), 0)
    top = layer_id == layers - 1

    def above(x):
        return pltpu.roll(x, layers - 1, 0)

    def below(x):
        return pltpu.roll(x, 1, 0)

    def prepare(r, low):
        h, w = fb[0, r], wet[r]
        high = 0.5 * (h + fb[0, r + 1]) * (w * wet[r + 1])
        across = 0.5 * (h + lane_next(h)) * (w * lane_next(jnp.broadcast_to(w, (layers, width))))
        total = jnp.where(top, h, h + above(h))
        upward = jnp.where(jnp.broadcast_to(w, total.shape) > 0.0, 2.0 / total, 0.0)
        inner = jnp.where(top, 0.0, upward)
        diagonal = 0.5 * h + low + high + lane_prev(across) + across + below(inner) + upward
        v = fb[3, r]
        y = fb[2, r]
        div = (
            0.5 * (fb[1, r + 1] - fb[1, r - 1])
            + 0.5 * (lane_next(y) - lane_prev(y))
            + (v - jnp.where(layer_id == 0, 0.0, below(v)))
        )
        force = -div * w
        inverse = jnp.where(diagonal == 0.0, 0.0, 1.0 / diagonal)
        ce[r] = high
        cn[r] = across
        up[r] = upward
        inv[r] = inverse
        z = force * inverse
        z0[r] = z
        return high, force, z

    def fold(x):
        return x[:half, :cols] + x[half:, :cols]

    first = REACH - ITERS
    ce[first - 1] = 0.5 * (fb[0, first - 1] + fb[0, first]) * (wet[first - 1] * wet[first])

    def prep_outer(r, low):
        return prepare(r, low)[0]

    def prep_inner(r, carry):
        low, acc = carry
        high, force, z = prepare(r, low)
        return high, acc + fold(force * z)

    zero = jnp.zeros((half, cols), jnp.float32)
    low = lax.fori_loop(first, R, prep_outer, ce[first - 1])
    low, m0 = lax.fori_loop(R, R + rows, prep_inner, (low, zero))
    lax.fori_loop(R + rows, R + rows + ITERS, prep_outer, low)

    def spread(z, r):
        x = z[r]
        c = cn[r]
        u = jnp.where(top, 0.0, up[r])
        return (
            ce[r - 1] * z[r - 1] + ce[r] * z[r + 1]
            + c * lane_next(x) + lane_prev(c * x)
            + u * above(x) + below(u * x)
        )

    def advance(z, target, reach):
        def outer(r, carry):
            target[r] = spread(z, r) * inv[r]
            return carry

        def inner(r, carry):
            odd, even = carry
            n = spread(z, r)
            y = n * inv[r]
            target[r] = y
            return odd + fold(z[r] * n), even + fold(y * n)

        lax.fori_loop(R - reach, R, outer, 0)
        sums = lax.fori_loop(R, R + rows, inner, (zero, zero))
        lax.fori_loop(R + rows, R + rows + reach, outer, 0)
        return sums

    m1, m2 = advance(z0, z1, 2)
    m3, m4 = advance(z1, z2, 1)
    m5 = lax.fori_loop(R, R + rows, lambda r, acc: acc + fold(z2[r] * spread(z2, r)), zero)

    part[0] = jnp.zeros((8, cols), jnp.float32)
    for k, m in enumerate((m0, m1, m2, m3, m4, m5)):
        part[0, k : k + 1, :] = jnp.sum(m, axis=0, keepdims=True)

    def everyone(count, slot, gather, send, recv, place):
        moves = [
            pltpu.make_async_remote_copy(
                src_ref=part.at[slot], dst_ref=gather.at[o - 1], send_sem=send.at[o - 1],
                recv_sem=recv.at[o - 1], device_id=place(o), device_id_type=MESH)
            for o in range(1, count)
        ]
        for move in moves:
            move.start()
        for move in moves:
            move.wait()
        return moves

    everyone(nx, 0, gather_x, send_gx, recv_gx, lambda o: (lax.rem(gx + o, nx), gy))
    total = part[0]
    for o in range(nx - 1):
        total = total + gather_x[o]
    part[1] = total
    everyone(ny, 1, gather_y, send_gy, recv_gy, lambda o: (gx, lax.rem(gy + o, ny)))
    for o in range(ny - 1):
        total = total + gather_y[o]
    sums = jnp.broadcast_to(jnp.sum(total, axis=1, keepdims=True), (8, width))
    m = [sums[k : k + 1, :] for k in range(6)]

    def dots(a, b, table):
        out = None
        for i in range(3):
            for j in range(3):
                if a[i] is not None and b[j] is not None:
                    t = a[i] * b[j] * table[i + j]
                    out = t if out is None else out + t
        return out

    shifted = [m[k] - m[k + 1] for k in range(5)]

    def plus(a, b, f):
        out = []
        for x, y in zip(a, b):
            out.append(x if y is None else (f * y if x is None else x + f * y))
        return out

    def image(d):
        moved = [None, d[0], d[1]]
        return [x if y is None else (None if x is None and y is None else (-y if x is None else x - y)) for x, y in zip(d, moved)]

    one = jnp.ones_like(m[0])
    direction = [one, None, None]
    residual = [one, None, None]
    pressure = [None, None, None]
    energy = m[0]
    for sweep in range(ITERS):
        bottom = dots(direction, direction, shifted)
        size = energy / bottom
        pressure = plus(pressure, direction, size)
        if sweep + 1 < ITERS:
            residual = plus(residual, image(direction), -size)
            fresh = dots(residual, residual, m)
            direction = plus(residual, direction, fresh / energy)
            energy = fresh

    def solve(r, carry):
        z0[r] = pressure[0] * z0[r] + pressure[1] * z1[r] + pressure[2] * z2[r]
        return carry

    lax.fori_loop(R - 1, R + rows + 1, solve, 0)

    def correct(r, carry):
        q, c = z0[r], cn[r]
        east = 0.5 * (ce[r] * (z0[r + 1] - q) + ce[r - 1] * (q - z0[r - 1]))
        slope = c * (lane_next(q) - q)
        north = 0.5 * (slope + lane_prev(slope))
        upward = up[r] * (jnp.where(top, 0.0, above(q)) - q)
        at = pl.ds(r - R, layers, stride=rows)
        depth_out[at, :] = fb[0, r, :, :cols]
        tracer_out[at, :] = fb[4, r, :, :cols]
        for n, push in enumerate((east, north, upward)):
            mom_out[n, at, :] = fb[1 + n, r, :, :cols] - push[:, :cols]
        return carry

    lax.fori_loop(R, R + rows, correct, 0)


def body(nx, ny, depth, momentum, tracer, cell_wet, tile_wet):
    layers, rows, cols = depth.shape
    assert TILE % rows == 0 and TILE % cols == 0 and cols == 128 and rows >= REACH
    f32 = jnp.float32
    tall = rows + 2 * REACH
    wide = 2 * cols
    half = layers // 2
    dma = pltpu.SemaphoreType.DMA
    vmem = pl.BlockSpec(memory_space=pltpu.VMEM)
    flat = jax.ShapeDtypeStruct((layers * rows, cols), f32)
    field = pltpu.VMEM((5, tall, layers, wide), f32)
    layer = pltpu.VMEM((tall, layers, wide), f32)
    packed = pltpu.VMEM((rows, half, cols), f32)
    halo = pltpu.VMEM((tall, half, cols), f32)
    pairs = [dma((2,))] * 6 + [dma((2, 2))] * 2 + [dma((nx - 1,))] * 2 + [dma((ny - 1,))] * 2
    new_depth, new_momentum, new_tracer = pl.pallas_call(
        functools.partial(kernel, nx, ny, rows, cols, layers),
        out_shape=(flat, jax.ShapeDtypeStruct((3, layers * rows, cols), f32), flat),
        in_specs=[pl.BlockSpec(memory_space=pltpu.SMEM)] + [vmem] * 4,
        out_specs=(vmem, vmem, vmem),
        scratch_shapes=[
            field, field, field,
            pltpu.VMEM((tall, 1, wide), f32),
            packed, packed, halo, halo,
            layer, layer, layer, layer, layer, layer, layer,
            pltpu.VMEM((2, 8, cols), f32),
            pltpu.VMEM((nx - 1, 8, cols), f32),
            pltpu.VMEM((ny - 1, 8, cols), f32),
            *pairs,
        ],
        compiler_params=pltpu.CompilerParams(
            collective_id=0, has_side_effects=True, vmem_limit_bytes=40 * 1024 * 1024
        ),
    )(
        tile_wet,
        depth.reshape(layers * rows, cols),
        momentum.reshape(3, layers * rows, cols),
        tracer.reshape(layers * rows, cols),
        cell_wet,
    )
    return (
        new_depth.reshape(depth.shape),
        new_momentum.reshape(momentum.shape),
        new_tracer.reshape(tracer.shape),
    )


def solution(mesh):
    placed = (
        P(None, "gx", "gy"),
        P(None, None, "gx", "gy"),
        P(None, "gx", "gy"),
        P("gx", "gy"),
        P(),
    )
    return jax.shard_map(
        functools.partial(body, mesh.shape["gx"], mesh.shape["gy"]),
        mesh=mesh,
        in_specs=placed,
        out_specs=(P(None, "gx", "gy"), P(None, None, "gx", "gy"), P(None, "gx", "gy")),
        check_vma=False,
    )
```

profile of v0, /device:TPU:0, one launch (start us, length us, event | category | flops | bytes accessed | tf_op | source)
XLA Modules:
  0.0 96.7 jit_solution(15303682733360979249)
XLA Ops:
  0.6 0.0 copy-start.4
  0.6 0.6 copy-done.4
  1.3 0.0 copy-start
  1.3 1.0 %copy-done = f32[3,16,16,128]{3,2,1,0:T(8,128)S(1)} copy-done((f32[3,16,16,128]{3,2,1,0:T(8,128)S(1)}, f32[3,16,16,128]{3,2,1,0:T(8,128)}, u32[]{:S(2)}) %copy-start) | copy-done | bytes 393240
  2.3 0.0 copy-start.1
  2.3 0.9 copy-done.1
  3.2 0.0 copy-start.2
  3.2 0.9 copy-done.2
  4.1 0.0 copy-start.3
  4.1 0.7 copy-done.3
  4.8 89.8 %shard_map.76 = (f32[256,128]{1,0:T(8,128)S(1)}, f32[3,256,128]{2,1,0:T(8,128)S(1)}, f32[256,128]{1,0:T(8,128)S(1)}) custom-call(s32[1,8]{1,0:T(1,128)S(1)} %copy-done.4, f32[256,128]{1,0:T(8,128)S(1)} %bitcast.10, f32[3,256,128]{2,1,0:T(8,128)S(1)} %bitcast.6, f32[256,128]{1,0:T(8,128)S(1)} %bitcast.11, s32[16,128]{1,0:T(8,128)S(1)} %copy-done.3), custom_call_target="tpu_custom_call" | custom-call | tf_op jit(solution)/shard_map/pallas_call | solution.py:409
  94.6 0.7 copy.11
  95.3 0.7 copy.12
  96.0 0.7 copy.13
Async XLA Ops:
  0.6 0.7 copy-start.4
  1.3 1.0 %copy-start = (f32[3,16,16,128]{3,2,1,0:T(8,128)S(1)}, f32[3,16,16,128]{3,2,1,0:T(8,128)}, u32[]{:S(2)}) copy-start(f32[3,16,16,128]{3,2,1,0:T(8,128)} %param.6) | copy-start | bytes 1179652
  2.3 0.9 copy-start.1
  3.2 0.9 copy-start.2
  4.1 0.7 copy-start.3
where the time goes:
time: 96.9 us; the launch traced here: 96.7 us
  Pallas kernels  89.8 us (93%)
  local copies, waits for them, and re-layouts  6.21 us (6%)
    pallas_call x1, Pallas kernels, body(): pl.pallas_call(functools.partial(kernel, nx, ny, rows, cols, layers), out...  89.8 us
    unnamed x13, local copies, waits for them, and re-layouts  6.21 us

commit v1 on v0

--- a/solution.py
+++ b/solution.py
@@ -23,8 +23,9 @@
 
 def hll(left, right, weight, normal):
     hl, hr = left[0], right[0]
-    ul, ur = left[normal] / hl, right[normal] / hr
-    al, ar = jnp.sqrt(gravity * hl), jnp.sqrt(gravity * hr)
+    rl, rr = lax.rsqrt(hl), lax.rsqrt(hr)
+    ul, ur = left[normal] * (rl * rl), right[normal] * (rr * rr)
+    al, ar = gravity**0.5 * (hl * rl), gravity**0.5 * (hr * rr)
     lower = jnp.minimum(jnp.minimum(ul - al, ur - ar), 0.0)
     upper = jnp.maximum(jnp.maximum(ul + al, ur + ar), 0.0)
     scale = weight / (upper - lower)
@@ -89,7 +90,7 @@
         fa[4, R + r, :, :cols] = tracer_ref[at, :]
         return carry
 
-    lax.fori_loop(0, rows, load_row, 0)
+    lax.fori_loop(0, rows, load_row, 0, unroll=4)
 
     lane = lax.broadcasted_iota(jnp.int32, (half, cols), 1)
 
@@ -108,7 +109,7 @@
         pack_r[r] = right
         return carry
 
-    lax.fori_loop(0, rows, pack_row, 0)
+    lax.fori_loop(0, rows, pack_row, 0, unroll=4)
 
     as_int = lambda flag: flag.astype(jnp.int32)
     corners = (as_int(has[-1]) + as_int(has[1])) * (as_int(side[-1]) + as_int(side[1]))
@@ -170,7 +171,7 @@
                 wet[r, :, cols:] = x[:1]
         return carry
 
-    lax.fori_loop(0, high_rows, unpack_row, 0)
+    lax.fori_loop(0, high_rows, unpack_row, 0, unroll=4)
 
     def transport(src, dst, lo, hi, keep):
         for part_of in range(2):
@@ -215,7 +216,7 @@
             a, b, c = usable(lo - 2), usable(lo - 1), usable(lo)
             _, left = sides(b, [y - x for x, y in zip(a, b)], [y - x for x, y in zip(b, c)])
             flux, left = row_face(lo - 1, left)
-            lax.fori_loop(lo, hi, step, (flux, left))
+            lax.fori_loop(lo, hi, step, (flux, left), unroll=4)
 
     transport(fa, fb, 2, high_rows - 2, None)
     transport(fb, fc, 4, high_rows - 4, 0.75)
@@ -271,7 +272,7 @@
 
     zero = jnp.zeros((half, cols), jnp.float32)
     low = lax.fori_loop(first, R, prep_outer, ce[first - 1])
-    low, m0 = lax.fori_loop(R, R + rows, prep_inner, (low, zero))
+    low, m0 = lax.fori_loop(R, R + rows, prep_inner, (low, zero), unroll=4)
     lax.fori_loop(R + rows, R + rows + ITERS, prep_outer, low)
 
     def spread(z, r):
@@ -297,13 +298,13 @@
             return odd + fold(z[r] * n), even + fold(y * n)
 
         lax.fori_loop(R - reach, R, outer, 0)
-        sums = lax.fori_loop(R, R + rows, inner, (zero, zero))
+        sums = lax.fori_loop(R, R + rows, inner, (zero, zero), unroll=4)
         lax.fori_loop(R + rows, R + rows + reach, outer, 0)
         return sums
 
     m1, m2 = advance(z0, z1, 2)
     m3, m4 = advance(z1, z2, 1)
-    m5 = lax.fori_loop(R, R + rows, lambda r, acc: acc + fold(z2[r] * spread(z2, r)), zero)
+    m5 = lax.fori_loop(R, R + rows, lambda r, acc: acc + fold(z2[r] * spread(z2, r)), zero, unroll=4)
 
     part[0] = jnp.zeros((8, cols), jnp.float32)
     for k, m in enumerate((m0, m1, m2, m3, m4, m5)):
@@ -373,7 +374,7 @@
         z0[r] = pressure[0] * z0[r] + pressure[1] * z1[r] + pressure[2] * z2[r]
         return carry
 
-    lax.fori_loop(R - 1, R + rows + 1, solve, 0)
+    lax.fori_loop(R - 1, R + rows + 1, solve, 0, unroll=6)
 
     def correct(r, carry):
         q, c = z0[r], cn[r]
@@ -388,7 +389,7 @@
             mom_out[n, at, :] = fb[1 + n, r, :, :cols] - push[:, :cols]
         return carry
 
-    lax.fori_loop(R, R + rows, correct, 0)
+    lax.fori_loop(R, R + rows, correct, 0, unroll=4)
 
 
 def body(nx, ny, depth, momentum, tracer, cell_wet, tile_wet):

time: 96.9 us -> 51.4 us (0.53)
  Pallas kernels: 89.8 us -> 44.3 us
    pallas_call x1, Pallas kernels: 89.8 us -> 44.3 us  [body(): pl.pallas_call(functools.partial(kernel, nx, ny, rows, cols, layers), out...]
where the time goes in v1:
time: 51.4 us; the launch traced here: 51.2 us
  Pallas kernels  44.3 us (86%)
  local copies, waits for them, and re-layouts  6.21 us (12%)
  between operations  0.65 us (1%)
    pallas_call x1, Pallas kernels, body(): pl.pallas_call(functools.partial(kernel, nx, ny, rows, cols, layers), out...  44.3 us
    unnamed x13, local copies, waits for them, and re-layouts  6.21 us

profile of v1, /device:TPU:0, one launch (start us, length us, event | category | flops | bytes accessed | tf_op | source)
XLA Modules:
  0.0 51.2 jit_solution(2222828241842948414)
XLA Ops:
  0.6 0.0 copy-start.4
  0.6 0.6 %copy-done.4 = s32[1,8]{1,0:T(1,128)S(1)} copy-done((s32[1,8]{1,0:T(1,128)S(1)}, s32[1,8]{1,0:T(1,128)}, u32[]{:S(2)}) %copy-start.4) | copy-done | bytes 56
  1.3 0.0 copy-start
  1.3 1.0 %copy-done = f32[3,16,16,128]{3,2,1,0:T(8,128)S(1)} copy-done((f32[3,16,16,128]{3,2,1,0:T(8,128)S(1)}, f32[3,16,16,128]{3,2,1,0:T(8,128)}, u32[]{:S(2)}) %copy-start) | copy-done | bytes 393240
  2.3 0.0 copy-start.1
  2.3 0.9 %copy-done.1 = f32[16,16,128]{2,1,0:T(8,128)S(1)} copy-done((f32[16,16,128]{2,1,0:T(8,128)S(1)}, f32[16,16,128]{2,1,0:T(8,128)}, u32[]{:S(2)}) %copy-start.1) | copy-done | bytes 131096
  3.2 0.0 copy-start.2
  3.2 0.9 %copy-done.2 = f32[16,16,128]{2,1,0:T(8,128)S(1)} copy-done((f32[16,16,128]{2,1,0:T(8,128)S(1)}, f32[16,16,128]{2,1,0:T(8,128)}, u32[]{:S(2)}) %copy-start.2) | copy-done | bytes 131096
  4.1 0.0 copy-start.3
  4.1 0.7 %copy-done.3 = s32[16,128]{1,0:T(8,128)S(1)} copy-done((s32[16,128]{1,0:T(8,128)S(1)}, s32[16,128]{1,0:T(8,128)}, u32[]{:S(2)}) %copy-start.3) | copy-done | bytes 8216
  4.8 44.3 %shard_map.76 = (f32[256,128]{1,0:T(8,128)S(1)}, f32[3,256,128]{2,1,0:T(8,128)S(1)}, f32[256,128]{1,0:T(8,128)S(1)}) custom-call(s32[1,8]{1,0:T(1,128)S(1)} %copy-done.4, f32[256,128]{1,0:T(8,128)S(1)} %bitcast.10, f32[3,256,128]{2,1,0:T(8,128)S(1)} %bitcast.6, f32[256,128]{1,0:T(8,128)S(1)} %bitcast.11, s32[16,128]{1,0:T(8,128)S(1)} %copy-done.3), custom_call_target="tpu_custom_call" | custom-call | tf_op jit(solution)/shard_map/pallas_call | solution.py:410
  49.1 0.7 %copy.11 = f32[16,16,128]{2,1,0:T(8,128)} copy(f32[16,16,128]{2,1,0:T(8,128)S(1)} %bitcast.9) | data formatting | bytes 262144
  49.8 0.7 %copy.12 = f32[3,16,16,128]{3,2,1,0:T(8,128)} copy(f32[3,16,16,128]{3,2,1,0:T(8,128)S(1)} %bitcast.7) | data formatting | bytes 786432
  50.5 0.7 %copy.13 = f32[16,16,128]{2,1,0:T(8,128)} copy(f32[16,16,128]{2,1,0:T(8,128)S(1)} %bitcast.8) | data formatting | bytes 262144
Async XLA Ops:
  0.6 0.7 %copy-start.4 = (s32[1,8]{1,0:T(1,128)S(1)}, s32[1,8]{1,0:T(1,128)}, u32[]{:S(2)}) copy-start(s32[1,8]{1,0:T(1,128)} %tile_ref.1) | copy-start | bytes 100
  1.3 1.0 %copy-start = (f32[3,16,16,128]{3,2,1,0:T(8,128)S(1)}, f32[3,16,16,128]{3,2,1,0:T(8,128)}, u32[]{:S(2)}) copy-start(f32[3,16,16,128]{3,2,1,0:T(8,128)} %param.6) | copy-start | bytes 1179652
  2.3 0.9 %copy-start.1 = (f32[16,16,128]{2,1,0:T(8,128)S(1)}, f32[16,16,128]{2,1,0:T(8,128)}, u32[]{:S(2)}) copy-start(f32[16,16,128]{2,1,0:T(8,128)} %param.5) | copy-start | bytes 393220
  3.2 0.9 %copy-start.2 = (f32[16,16,128]{2,1,0:T(8,128)S(1)}, f32[16,16,128]{2,1,0:T(8,128)}, u32[]{:S(2)}) copy-start(f32[16,16,128]{2,1,0:T(8,128)} %param.7) | copy-start | bytes 393220
  4.1 0.7 %copy-start.3 = (s32[16,128]{1,0:T(8,128)S(1)}, s32[16,128]{1,0:T(8,128)}, u32[]{:S(2)}) copy-start(s32[16,128]{1,0:T(8,128)} %wet_ref.1) | copy-start | bytes 24580

commit v2 on v1

--- a/solution.py
+++ b/solution.py
@@ -47,8 +47,9 @@
 
 def kernel(
     nx, ny, rows, cols, layers,
-    tile_ref, depth_ref, mom_ref, tracer_ref, wet_ref,
+    tile_hbm, depth_hbm, mom_hbm, tracer_hbm, wet_hbm,
     depth_out, mom_out, tracer_out,
+    staged, wet_ref, tile_ref, load_sem, pushes,
     fa, fb, fc, wet, pack_l, pack_r, halo_l, halo_r,
     ce, cn, up, inv, z0, z1, z2, part, gather_x, gather_y,
     send_row, recv_row, send_wet, recv_wet, send_col, recv_col,
@@ -60,7 +61,16 @@
     half = layers // 2
     gx, gy = lax.axis_index("gx"), lax.axis_index("gy")
 
-    fa[...] = jnp.zeros_like(fa)
+    loads = [
+        pltpu.make_async_copy(wet_hbm, wet_ref, load_sem.at[0]),
+        pltpu.make_async_copy(depth_hbm, staged.at[0], load_sem.at[1]),
+        pltpu.make_async_copy(mom_hbm, staged.at[pl.ds(1, 3)], load_sem.at[2]),
+        pltpu.make_async_copy(tracer_hbm, staged.at[4], load_sem.at[3]),
+        pltpu.make_async_copy(tile_hbm, tile_ref, load_sem.at[4]),
+    ]
+    for load in loads:
+        load.start()
+
     wet[...] = jnp.zeros_like(wet)
     halo_l[...] = jnp.zeros_like(halo_l)
     halo_r[...] = jnp.zeros_like(halo_r)
@@ -78,38 +88,24 @@
             def _(dx=dx, dy=dy):
                 pl.semaphore_signal(barrier, inc=1, device_id=(gx + dx, gy + dy), device_id_type=MESH)
 
+    for dx, start in ((-1, 0), (1, R + rows)):
+        @pl.when(jnp.logical_not(has[dx]))
+        def _(start=start):
+            fa[:, start : start + R, :, :cols] = jnp.zeros((5, R, layers, cols), jnp.float32)
+
+    for load in loads:
+        load.wait()
     tile = tile_ref[(gx * rows) // TILE, (gy * cols) // TILE].astype(jnp.float32)
     for r in range(rows):
         wet[R + r, :, :cols] = wet_ref[r : r + 1, :].astype(jnp.float32) * tile
 
     def load_row(r, carry):
         at = pl.ds(r, layers, stride=rows)
-        fa[0, R + r, :, :cols] = depth_ref[at, :]
-        for n in range(3):
-            fa[1 + n, R + r, :, :cols] = mom_ref[n, at, :]
-        fa[4, R + r, :, :cols] = tracer_ref[at, :]
+        for f in range(5):
+            fa[f, R + r, :, :cols] = staged[f, at, :]
         return carry
 
     lax.fori_loop(0, rows, load_row, 0, unroll=4)
-
-    lane = lax.broadcasted_iota(jnp.int32, (half, cols), 1)
-
-    def pack_row(r, carry):
-        left = jnp.zeros((half, cols), jnp.float32)
-        right = left
-        for s in range(11):
-            if s < 10:
-                x = fa[s % 5, R + r, (s // 5) * half : (s // 5 + 1) * half, :cols]
-            else:
-                x = jnp.broadcast_to(wet[R + r, :, :cols], (half, cols))
-            mask = jnp.logical_and(lane >= SEG * s, lane < SEG * s + R)
-            left = jnp.where(mask, pltpu.roll(x, SEG * s, 1) if s else x, left)
-            right = jnp.where(mask, pltpu.roll(x, (SEG * s + R) % cols, 1), right)
-        pack_l[r] = left
-        pack_r[r] = right
-        return carry
-
-    lax.fori_loop(0, rows, pack_row, 0, unroll=4)
 
     as_int = lambda flag: flag.astype(jnp.int32)
     corners = (as_int(has[-1]) + as_int(has[1])) * (as_int(side[-1]) + as_int(side[1]))
@@ -149,15 +145,44 @@
             copies.append((jnp.logical_and(has[dx], side[dy]),
                            pltpu.make_async_remote_copy(recv_sem=recv_cor.at[i, j], **args),
                            pltpu.make_async_remote_copy(recv_sem=recv_cor.at[1 - i, 1 - j], **args)))
-    for cond, go, come in copies:
-        @pl.when(cond)
-        def _(go=go):
-            go.start()
-    for cond, go, come in copies:
-        @pl.when(cond)
-        def _(go=go, come=come):
-            go.wait_send()
-            come.wait_recv()
+    def begin(group):
+        for cond, go, come in group:
+            @pl.when(cond)
+            def _(go=go):
+                go.start()
+
+    def finish(group):
+        for cond, go, come in group:
+            @pl.when(cond)
+            def _(go=go, come=come):
+                go.wait_send()
+                come.wait_recv()
+
+    tall_copies, edge_copies, corner_copies = copies[:4], [copies[4], copies[7]], copies[5:7] + copies[8:]
+    begin(tall_copies)
+
+    lane = lax.broadcasted_iota(jnp.int32, (half, cols), 1)
+
+    def pack_row(r, carry):
+        left = jnp.zeros((half, cols), jnp.float32)
+        right = left
+        for s in range(11):
+            if s < 10:
+                x = fa[s % 5, R + r, (s // 5) * half : (s // 5 + 1) * half, :cols]
+            else:
+                x = jnp.broadcast_to(wet[R + r, :, :cols], (half, cols))
+            mask = jnp.logical_and(lane >= SEG * s, lane < SEG * s + R)
+            left = jnp.where(mask, pltpu.roll(x, SEG * s, 1) if s else x, left)
+            right = jnp.where(mask, pltpu.roll(x, (SEG * s + R) % cols, 1), right)
+        pack_l[r] = left
+        pack_r[r] = right
+        return carry
+
+    lax.fori_loop(0, rows, pack_row, 0, unroll=4)
+
+    begin(edge_copies)
+    begin(corner_copies)
+    finish(edge_copies)
 
     def unpack_row(r, carry):
         fr, fl = halo_r[r], halo_l[r]
@@ -171,9 +196,9 @@
                 wet[r, :, cols:] = x[:1]
         return carry
 
-    lax.fori_loop(0, high_rows, unpack_row, 0, unroll=4)
-
-    def transport(src, dst, lo, hi, keep):
+    lax.fori_loop(R, R + rows, unpack_row, 0, unroll=4)
+
+    def transport(src, dst, lo, hi, keep, unroll=4):
         for part_of in range(2):
             cut = slice(part_of * half, (part_of + 1) * half)
 
@@ -216,9 +241,15 @@
             a, b, c = usable(lo - 2), usable(lo - 1), usable(lo)
             _, left = sides(b, [y - x for x, y in zip(a, b)], [y - x for x, y in zip(b, c)])
             flux, left = row_face(lo - 1, left)
-            lax.fori_loop(lo, hi, step, (flux, left), unroll=4)
-
-    transport(fa, fb, 2, high_rows - 2, None)
+            lax.fori_loop(lo, hi, step, (flux, left), unroll=unroll)
+
+    transport(fa, fb, R + 2, R + rows - 2, None)
+    finish(tall_copies)
+    finish(corner_copies)
+    lax.fori_loop(0, R, unpack_row, 0, unroll=5)
+    lax.fori_loop(R + rows, high_rows, unpack_row, 0, unroll=5)
+    transport(fa, fb, 2, R + 2, None, 5)
+    transport(fa, fb, R + rows - 2, high_rows - 2, None, 5)
     transport(fb, fc, 4, high_rows - 4, 0.75)
     transport(fc, fb, 6, high_rows - 6, 1.0 / 3.0)
 
@@ -271,9 +302,9 @@
         return high, acc + fold(force * z)
 
     zero = jnp.zeros((half, cols), jnp.float32)
-    low = lax.fori_loop(first, R, prep_outer, ce[first - 1])
+    low = lax.fori_loop(first, R, prep_outer, ce[first - 1], unroll=True)
     low, m0 = lax.fori_loop(R, R + rows, prep_inner, (low, zero), unroll=4)
-    lax.fori_loop(R + rows, R + rows + ITERS, prep_outer, low)
+    lax.fori_loop(R + rows, R + rows + ITERS, prep_outer, low, unroll=True)
 
     def spread(z, r):
         x = z[r]
@@ -297,9 +328,9 @@
             target[r] = y
             return odd + fold(z[r] * n), even + fold(y * n)
 
-        lax.fori_loop(R - reach, R, outer, 0)
+        lax.fori_loop(R - reach, R, outer, 0, unroll=True)
         sums = lax.fori_loop(R, R + rows, inner, (zero, zero), unroll=4)
-        lax.fori_loop(R + rows, R + rows + reach, outer, 0)
+        lax.fori_loop(R + rows, R + rows + reach, outer, 0, unroll=True)
         return sums
 
     m1, m2 = advance(z0, z1, 2)
@@ -309,6 +340,19 @@
     part[0] = jnp.zeros((8, cols), jnp.float32)
     for k, m in enumerate((m0, m1, m2, m3, m4, m5)):
         part[0, k : k + 1, :] = jnp.sum(m, axis=0, keepdims=True)
+
+    def push_of(k, z):
+        def row(r, carry):
+            q, c = z[r], cn[r]
+            east = 0.5 * (ce[r] * (z[r + 1] - q) + ce[r - 1] * (q - z[r - 1]))
+            slope = c * (lane_next(q) - q)
+            north = 0.5 * (slope + lane_prev(slope))
+            upward = up[r] * (jnp.where(top, 0.0, above(q)) - q)
+            for n, push in enumerate((east, north, upward)):
+                pushes[k, n, r - R] = push[:, :cols]
+            return carry
+
+        lax.fori_loop(R, R + rows, row, 0, unroll=4)
 
     def everyone(count, slot, gather, send, recv, place):
         moves = [
@@ -319,19 +363,31 @@
         ]
         for move in moves:
             move.start()
-        for move in moves:
-            move.wait()
         return moves
 
-    everyone(nx, 0, gather_x, send_gx, recv_gx, lambda o: (lax.rem(gx + o, nx), gy))
+    def plain_out(r, carry):
+        at = pl.ds(r - R, layers, stride=rows)
+        depth_out[at, :] = fb[0, r, :, :cols]
+        tracer_out[at, :] = fb[4, r, :, :cols]
+        return carry
+
+    moves = everyone(nx, 0, gather_x, send_gx, recv_gx, lambda o: (lax.rem(gx + o, nx), gy))
+    push_of(0, z0)
+    push_of(1, z1)
+    for move in moves:
+        move.wait()
     total = part[0]
     for o in range(nx - 1):
         total = total + gather_x[o]
     part[1] = total
-    everyone(ny, 1, gather_y, send_gy, recv_gy, lambda o: (gx, lax.rem(gy + o, ny)))
+    moves = everyone(ny, 1, gather_y, send_gy, recv_gy, lambda o: (gx, lax.rem(gy + o, ny)))
+    push_of(2, z2)
+    lax.fori_loop(R, R + rows, plain_out, 0, unroll=4)
+    for move in moves:
+        move.wait()
     for o in range(ny - 1):
         total = total + gather_y[o]
-    sums = jnp.broadcast_to(jnp.sum(total, axis=1, keepdims=True), (8, width))
+    sums = jnp.broadcast_to(jnp.sum(total, axis=1, keepdims=True), (8, cols))
     m = [sums[k : k + 1, :] for k in range(6)]
 
     def dots(a, b, table):
@@ -370,23 +426,12 @@
             direction = plus(residual, direction, fresh / energy)
             energy = fresh
 
-    def solve(r, carry):
-        z0[r] = pressure[0] * z0[r] + pressure[1] * z1[r] + pressure[2] * z2[r]
-        return carry
-
-    lax.fori_loop(R - 1, R + rows + 1, solve, 0, unroll=6)
-
     def correct(r, carry):
-        q, c = z0[r], cn[r]
-        east = 0.5 * (ce[r] * (z0[r + 1] - q) + ce[r - 1] * (q - z0[r - 1]))
-        slope = c * (lane_next(q) - q)
-        north = 0.5 * (slope + lane_prev(slope))
-        upward = up[r] * (jnp.where(top, 0.0, above(q)) - q)
         at = pl.ds(r - R, layers, stride=rows)
-        depth_out[at, :] = fb[0, r, :, :cols]
-        tracer_out[at, :] = fb[4, r, :, :cols]
-        for n, push in enumerate((east, north, upward)):
-            mom_out[n, at, :] = fb[1 + n, r, :, :cols] - push[:, :cols]
+        for n in range(3):
+            push = pressure[0] * pushes[0, n, r - R]
+            push = push + pressure[1] * pushes[1, n, r - R] + pressure[2] * pushes[2, n, r - R]
+            mom_out[n, at, :] = fb[1 + n, r, :, :cols] - push
         return carry
 
     lax.fori_loop(R, R + rows, correct, 0, unroll=4)
@@ -410,9 +455,14 @@
     new_depth, new_momentum, new_tracer = pl.pallas_call(
         functools.partial(kernel, nx, ny, rows, cols, layers),
         out_shape=(flat, jax.ShapeDtypeStruct((3, layers * rows, cols), f32), flat),
-        in_specs=[pl.BlockSpec(memory_space=pltpu.SMEM)] + [vmem] * 4,
+        in_specs=[pl.BlockSpec(memory_space=pltpu.HBM)] * 5,
         out_specs=(vmem, vmem, vmem),
         scratch_shapes=[
+            pltpu.VMEM((5, layers * rows, cols), f32),
+            pltpu.VMEM((rows, cols), jnp.int32),
+            pltpu.SMEM(tile_wet.shape, jnp.int32),
+            dma((5,)),
+            pltpu.VMEM((3, 3, rows, layers, cols), f32),
             field, field, field,
             pltpu.VMEM((tall, 1, wide), f32),
             packed, packed, halo, halo,
@@ -423,7 +473,7 @@
             *pairs,
         ],
         compiler_params=pltpu.CompilerParams(
-            collective_id=0, has_side_effects=True, vmem_limit_bytes=40 * 1024 * 1024
+            collective_id=0, has_side_effects=True, vmem_limit_bytes=56 * 1024 * 1024
         ),
     )(
         tile_wet,

time: 51.4 us -> 47.6 us (0.926)
  local copies, waits for them, and re-layouts: 6.21 us -> 4.03 us
  Pallas kernels: 44.3 us -> 42.7 us
    unnamed x13 -> x5, local copies, waits for them, and re-layouts: 6.21 us -> 4.03 us
    pallas_call x1, Pallas kernels: 44.3 us -> 42.7 us  [body(): pl.pallas_call(functools.partial(kernel, nx, ny, rows, cols, layers), out...]
where the time goes in v2:
time: 47.6 us; the launch traced here: 47.4 us
  Pallas kernels  42.7 us (90%)
  local copies, waits for them, and re-layouts  4.03 us (8%)
  between operations  0.64 us (1%)
    pallas_call x1, Pallas kernels, body(): pl.pallas_call(functools.partial(kernel, nx, ny, rows, cols, layers), out...  42.7 us
    unnamed x5, local copies, waits for them, and re-layouts  4.03 us

profile of v2, /device:TPU:0, one launch (start us, length us, event | category | flops | bytes accessed | tf_op | source)
XLA Modules:
  0.0 47.4 jit_solution(6431912310996956145)
XLA Ops:
  0.6 42.7 %shard_map.76 = (f32[256,128]{1,0:T(8,128)}, f32[3,256,128]{2,1,0:T(8,128)}, f32[256,128]{1,0:T(8,128)}) custom-call(s32[1,8]{1,0:T(1,128)} %tile_hbm.1, f32[256,128]{1,0:T(8,128)} %bitcast.10, f32[3,256,128]{2,1,0:T(8,128)} %bitcast.6, f32[256,128]{1,0:T(8,128)} %bitcast.11, s32[16,128]{1,0:T(8,128)} %wet_hbm.1), custom_call_target="tpu_custom_call" | custom-call | tf_op jit(solution)/shard_map/pallas_call | solution.py:455
  43.3 1.6 %copy.11 = f32[16,16,128]{2,1,0:T(8,128)} copy(f32[16,16,128]{2,1,0:T(8,128)} %bitcast.9) | data formatting | bytes 262144
  44.9 0.0 copy-start
  44.9 1.8 %copy.12 = f32[3,16,16,128]{3,2,1,0:T(8,128)} copy(f32[3,16,16,128]{3,2,1,0:T(8,128)} %bitcast.7) | data formatting | bytes 786432
  46.7 0.0 copy-done
  46.7 0.7 %copy.13 = f32[16,16,128]{2,1,0:T(8,128)} copy(f32[16,16,128]{2,1,0:T(8,128)S(1)} %bitcast.8) | data formatting | bytes 262144
Async XLA Ops:
  44.9 1.8 %copy-start = (f32[256,128]{1,0:T(8,128)S(1)}, f32[256,128]{1,0:T(8,128)}, u32[]{:S(2)}) copy-start(f32[256,128]{1,0:T(8,128)} %get-tuple-element.8) | copy-start | bytes 393220
